TPU v7x, 32 devices: a whole 2x2x4 slice. The times are simulated.
32 devices in a mesh: row: 8 (over z, core), col: 4 (over y, x).
Axes of the slice: x: 2, y: 2, z: 4, core: 2. Of those that a mesh axis runs over, the one named last changes fastest.
Arguments:
- density: bfloat16 [8192, 8192], P('row', 'col'), may hold values from -6 to 6
- listed: int32 [64, 64], P('row', 'col'), may hold values 0 or 1
- three_centre: bfloat16 [128, 512, 512], P(('row', 'col')), may hold values from -0.25 to 0.25
Outputs:
- exchange_diag: float32 [8192, 512], P('row', 'col')
- exchange_density: bfloat16 [8192, 8192], P('row', 'col')
All inputs are finite; a program needn't handle non-finite values. No bound on the sum of `listed` on one device may be relied on, other than what follows from the above.
Results may differ from a plain program's by a relative error of at most 0.0058.
Values may be sent and summed in bfloat16 or wider, within the bound.
A program may use at most 64 MiB of HBM per device.

v0:
```python
import jax
import jax.numpy as jnp
from jax import lax
from jax.sharding import PartitionSpec as P

TILE = 128
W = 512


def from_root(value, axis, root):
    mine = lax.axis_index(axis) == root
    return lax.psum(jnp.where(mine, value, jnp.zeros_like(value)), axis)


def partner_2(block, axis, stride):
    count = lax.axis_size(axis)
    route = []
    for low in range(count):
        high = low | 1 << stride
        if high != low and high < count:
            route += [(low, high), (high, low)]
    return lax.ppermute(block, axis, route)


def halve_rows(values, row_index, levels, sender):
    for bit_level in reversed(range(levels)):
        middle = values.shape[0] // 2
        lower_half = row_index // 2**bit_level % 2 == 0
        kept_rows = jnp.where(lower_half, values[:middle], values[middle:])
        sent_rows = jnp.where(lower_half, values[middle:], values[:middle])
        values = kept_rows + sender(sent_rows, bit_level)
    return values


def per_device(density, listed, three_centre):
    tile_rows = listed.shape[0]
    tile_cols = listed.shape[1]
    quad_tiles = max(tile_rows, 4)
    groups_dev = quad_tiles // 4
    aux_count = three_centre.shape[0]
    col_count = lax.axis_size("col")
    row_index = lax.axis_index("row")
    col_index = lax.axis_index("col")
    masked = (
        density.reshape(tile_rows, TILE, tile_cols, TILE)
        * listed[:, None, :, None].astype(jnp.bfloat16)
    ).reshape(tile_rows * TILE, tile_cols * TILE)
    quad_start = row_index * tile_rows // quad_tiles * quad_tiles
    col_offset = quad_start % tile_cols * TILE
    portion = lax.dynamic_slice_in_dim(masked, col_offset, quad_tiles * TILE, 1)
    diagonal = from_root(portion, "col", quad_start // tile_cols)
    joined = jnp.concatenate([diagonal, masked], axis=1)
    levels = (quad_tiles // tile_rows).bit_length() - 1
    for bit_level in range(levels):
        partner = partner_2(joined, "row", bit_level)
        lower_half = row_index // 2**bit_level % 2 == 0
        joined = jnp.where(
            lower_half,
            jnp.concatenate([joined, partner], axis=0),
            jnp.concatenate([partner, joined], axis=0),
        )
    quad_block = joined[:, : quad_tiles * TILE]
    quad_density = joined[:, quad_tiles * TILE :]
    group_ids = jnp.arange(groups_dev, dtype=jnp.int32)
    exchange_quad = jnp.zeros((groups_dev, W, W), jnp.float32)
    for aux_slot in range(aux_count):
        group_slot = (col_index * aux_count + aux_slot) % groups_dev
        density_sub = lax.dynamic_slice(quad_block, (group_slot * W, group_slot * W), (W, W))
        aux_block = three_centre[aux_slot]
        half_product = jnp.dot(aux_block, density_sub, preferred_element_type=jnp.float32).astype(
            jnp.bfloat16
        )
        contribution = lax.dot_general(
            half_product, aux_block, (((1,), (1,)), ((), ())), preferred_element_type=jnp.float32
        )
        exchange_quad = exchange_quad + jnp.where(
            (group_ids == group_slot)[:, None, None], contribution[None], 0.0
        )
    aux_group = aux_count * col_count * 4 // tile_rows
    exchange_quad = (exchange_quad * aux_group ** (-0.5)).reshape(quad_tiles * TILE, W)
    column_share = lax.psum_scatter(exchange_quad, "col", scatter_dimension=1, tiled=True)
    exchange_diag = halve_rows(
        column_share,
        row_index,
        levels,
        lambda sent_rows, bit_level: partner_2(sent_rows, "row", bit_level),
    )
    fock_rounded = lax.all_gather(exchange_diag.astype(jnp.bfloat16), "col", axis=1, tiled=True)
    rows_here = tile_rows * TILE
    segment_rows = min(rows_here, W)
    segment_count = rows_here // segment_rows
    within_quad = (row_index * tile_rows - quad_start) * TILE
    products = []
    for segment in range(segment_count):
        group_position = (within_quad + segment * segment_rows) // W
        dens_rows = lax.dynamic_slice_in_dim(quad_density, group_position * W, W, 0)
        fock_part = fock_rounded[segment * segment_rows : (segment + 1) * segment_rows]
        products.append(
            jnp.dot(fock_part, dens_rows, preferred_element_type=jnp.float32) * W ** (-0.5)
        )
    exchange_density = jnp.concatenate(products, axis=0).astype(jnp.bfloat16)
    return (exchange_diag, exchange_density)


def solution(mesh):
    placed = (P("row", "col"), P("row", "col"), P(("row", "col"), None, None))
    return jax.shard_map(
        per_device,
        mesh=mesh,
        in_specs=placed,
        out_specs=(P("row", "col"), P("row", "col")),
        check_vma=False,
    )
```

profile of v0, /device:TPU:0, one launch (start us, length us, event | category | flops | bytes accessed | tf_op | source)
XLA Modules:
  0.0 177.6 jit_solution(2169298815006904635)
XLA Ops:
  7.2 0.0 all-reduce.2.cloned.1.call-start
  7.3 0.7 convert_element_type.24
  7.9 0.0 copy-start.2
  8.0 0.6 mul.68
  8.6 1.6 copy-done.2
  10.1 0.9 bitcast_multiply_fusion
  11.0 0.0 copy-start
  11.1 2.0 %copy-done = bf16[1024,2048]{1,0:T(8,128)(2,1)} copy-done((bf16[1024,2048]{1,0:T(8,128)(2,1)}, bf16[1024,2048]{1,0:T(8,128)(2,1)S(1)}, u32[]{:S(2)}) %copy-start) | copy-done | bytes 4194328
  13.1 1.9 %dynamic-slice_select_fusion = bf16[1024,1024]{1,0:T(8,128)(2,1)} fusion(bf16[1024,2048]{1,0:T(8,128)(2,1)S(1)} %bitcast_multiply_fusion, s32[]{:T(128)S(6)} %select_n.91, pred[]{:T(512)S(6)} %eq.51), kind=kLoop, calls=%fused_computation.14 | loop fusion | flops 1048576 | bytes 4194309 | tf_op jit(solution)/shard_map/jit(_where)/select_n | solution.py:12
  14.9 0.0 copy-start.3
  14.9 0.0 all-reduce.2.cloned.1.call-update
  14.9 0.0 reduce-scatter.2.cloned.1.call-start
  15.1 0.1 broadcast_in_dim.101
  15.2 0.1 broadcast_in_dim.106
  15.3 0.1 broadcast_in_dim.96
  15.4 0.1 broadcast_in_dim.89
  15.5 71.9 %all-reduce.2.cloned.1.call-done = bf16[1024,1024]{1,0:T(8,128)(2,1)} async-done(((bf16[1024,1024]{1,0:T(8,128)(2,1)}), bf16[1024,1024]{1,0:T(8,128)(2,1)}) %all-reduce.2.cloned.1.call-update) | async-done | bytes 2097168 | tf_op jit(solution)/shard_map/psum | solution.py:12
  87.3 0.0 copy-done.3
  87.3 1.9 %fusion.7 = f32[512,512]{1,0:T(8,128)S(1)} fusion(bf16[4,512,512]{2,1,0:T(8,128)(2,1)S(1)} %copy-done.3, bf16[1024,1024]{1,0:T(8,128)(2,1)} %all-reduce.2.cloned.1.call-done, s32[]{:T(128)S(6)} %select_n.96), kind=kOutput, calls=%fused_computation.20 | convolution fusion | flops 537133056 | bytes 2621444 | tf_op jit(solution)/shard_map/dot_general | solution.py:73
  89.2 2.2 %fusion.8 = f32[512,512]{1,0:T(8,128)S(1)} fusion(bf16[4,512,512]{2,1,0:T(8,128)(2,1)} %param.5, bf16[1024,1024]{1,0:T(8,128)(2,1)} %all-reduce.2.cloned.1.call-done, s32[]{:T(128)S(6)} %select_n.99), kind=kOutput, calls=%fused_computation.21 | convolution fusion | flops 537133056 | bytes 2621444 | tf_op jit(solution)/shard_map/dot_general | solution.py:73
  91.5 2.2 %fusion.6 = f32[512,512]{1,0:T(8,128)S(1)} fusion(bf16[4,512,512]{2,1,0:T(8,128)(2,1)} %param.5, bf16[1024,1024]{1,0:T(8,128)(2,1)} %all-reduce.2.cloned.1.call-done, s32[]{:T(128)S(6)} %select_n.93), kind=kOutput, calls=%fused_computation.19 | convolution fusion | flops 537133056 | bytes 2621444 | tf_op jit(solution)/shard_map/dot_general | solution.py:73
  93.7 3.2 %fusion.9 = f32[512,512]{1,0:T(8,128)} fusion(bf16[4,512,512]{2,1,0:T(8,128)(2,1)} %param.5, bf16[1024,1024]{1,0:T(8,128)(2,1)} %all-reduce.2.cloned.1.call-done, s32[]{:T(128)S(6)} %select_n.102), kind=kOutput, calls=%fused_computation.22 | convolution fusion | flops 537133056 | bytes 2621444 | tf_op jit(solution)/shard_map/dot_general | solution.py:73
  96.9 3.3 %fusion.1 = f32[1024,512]{1,0:T(8,128)} fusion(f32[512,512]{1,0:T(8,128)} %fusion.9, f32[512,512]{1,0:T(8,128)S(1)} %fusion.8, f32[512,512]{1,0:T(8,128)S(1)} %fusion.7, f32[512,512]{1,0:T(8,128)S(1)} %fusion.6, pred[1024]{0:T(1024)(128)(4,1)S(1)} %broadcast_in_dim.107, pred[1024]{0:T(1024)(128)(4,1)S(1)} %broadcast_in_dim.102, ...), kind=kLoop, calls=%fused_computation.6 | loop fusion | flops 4194304 | bytes 6295552 | tf_op jit(solution)/shard_map/mul | solution.py:80
  100.2 0.0 reduce-scatter.2.cloned.1.call-update
  100.2 0.0 all-gather.2.cloned.1.call-start
  100.3 35.3 %reduce-scatter.2.cloned.1.call-done = f32[1024,128]{1,0:T(8,128)} async-done(((f32[1024,512]{1,0:T(8,128)}), f32[1024,128]{1,0:T(8,128)}) %reduce-scatter.2.cloned.1.call-update) | async-done | bytes 524304 | tf_op jit(solution)/shard_map/reduce_scatter | solution.py:81
  135.6 1.8 %convert_element_type.29 = bf16[1024,128]{1,0:T(8,128)(2,1)} convert(f32[1024,128]{1,0:T(8,128)} %reduce-scatter.2.cloned.1.call-done) | non-fusion elementwise | flops 131072 | bytes 786432 | tf_op jit(solution)/shard_map/convert_element_type | solution.py:88
  137.3 0.0 all-gather.2.cloned.1.call-update
  137.4 26.5 %all-gather.2.cloned.1.call-done = bf16[1024,512]{1,0:T(8,128)(2,1)} async-done(((bf16[1024,128]{1,0:T(8,128)(2,1)}), bf16[1024,512]{1,0:T(8,128)(2,1)}) %all-gather.2.cloned.1.call-update) | async-done | bytes 1048592 | tf_op jit(solution)/shard_map/all_gather | solution.py:88
  163.9 0.0 copy-start.1
  163.9 0.0 copy-start.4
  163.9 3.2 %multiply_convert_fusion.1 = bf16[512,2048]{1,0:T(8,128)(2,1)S(1)} fusion(bf16[1024,2048]{1,0:T(8,128)(2,1)} %copy-done, s32[]{:T(128)S(6)} %select_n.105, bf16[1024,512]{1,0:T(8,128)(2,1)} %all-gather.2.cloned.1.call-done), kind=kOutput, calls=%fused_computation.3 | convolution fusion | flops 1075838976 | bytes 4718596 | tf_op jit(solution)/shard_map/dot_general | solution.py:99
  167.1 0.0 copy-done.1
  167.1 0.1 copy-done.4
  167.2 1.3 multiply_convert_fusion
  168.4 2.6 %pad_maximum_fusion = bf16[1024,2048]{1,0:T(8,128)(2,1)} fusion(bf16[512,2048]{1,0:T(8,128)(2,1)S(1)} %multiply_convert_fusion, bf16[512,2048]{1,0:T(8,128)(2,1)S(1)} %multiply_convert_fusion.1), kind=kLoop, calls=%fused_computation.1 | loop fusion | flops 8388608 | bytes 8388608 | tf_op jit(solution)/shard_map/concatenate | solution.py:101
  (8 shorter events, 0.1 us)
Async XLA Ops:
  7.2 80.1 %all-reduce.2.cloned.1.call-start = ((), (), s32[]{:S(2)}) async-start(), calls=%async_computation.1 | async-start | bytes 4194304 | tf_op jit(solution)/shard_map/psum | solution.py:12
  7.9 2.2 %copy-start.2 = (bf16[1024,2048]{1,0:T(8,128)(2,1)S(1)}, bf16[1024,2048]{1,0:T(8,128)(2,1)}, u32[]{:S(2)}) copy-start(bf16[1024,2048]{1,0:T(8,128)(2,1)} %param.3) | copy-start | bytes 12582916
  11.0 2.0 %copy-start = (bf16[1024,2048]{1,0:T(8,128)(2,1)}, bf16[1024,2048]{1,0:T(8,128)(2,1)S(1)}, u32[]{:S(2)}) copy-start(bf16[1024,2048]{1,0:T(8,128)(2,1)S(1)} %bitcast_multiply_fusion) | copy-start | bytes 12582916
  14.9 72.4 %copy-start.3 = (bf16[4,512,512]{2,1,0:T(8,128)(2,1)S(1)}, bf16[4,512,512]{2,1,0:T(8,128)(2,1)}, u32[]{:S(2)}) copy-start(bf16[4,512,512]{2,1,0:T(8,128)(2,1)} %param.5) | copy-start | bytes 6291460
  14.9 120.6 %reduce-scatter.2.cloned.1.call-start = ((), (), s32[]{:S(2)}) async-start(), calls=%async_computation.2 | async-start | bytes 2621440 | tf_op jit(solution)/shard_map/reduce_scatter | solution.py:81
  100.2 63.7 %all-gather.2.cloned.1.call-start = ((), (), s32[]{:S(2)}) async-start(), calls=%async_computation.3 | async-start | bytes 1310720 | tf_op jit(solution)/shard_map/all_gather | solution.py:88
  163.9 3.2 %copy-start.1 = (bf16[1024,2048]{1,0:T(8,128)(2,1)S(1)}, bf16[1024,2048]{1,0:T(8,128)(2,1)}, u32[]{:S(2)}) copy-start(bf16[1024,2048]{1,0:T(8,128)(2,1)} %copy-done) | copy-start | bytes 12582916
  163.9 3.3 %copy-start.4 = (bf16[1024,512]{1,0:T(8,128)(2,1)S(1)}, bf16[1024,512]{1,0:T(8,128)(2,1)}, u32[]{:S(2)}) copy-start(bf16[1024,512]{1,0:T(8,128)(2,1)} %all-gather.2.cloned.1.call-done) | copy-start | bytes 3145732
Sparse Core Ops, SparseCore 0:
  15.1 72.1 all-reduce.1
  100.3 35.1 reduce-scatter.1
  137.5 26.3 all-gather.1
where the time goes:
time: 178 us
  waiting for transfers between devices  134 us (75%)
  matrix products  14 us (8%)
  between operations  14 us (8%)
  other arithmetic  11.1 us (6%)
  local copies, waits for them, and re-layouts  4.68 us (3%)
    psum x1, waiting for transfers between devices, from_root(): return lax.psum(jnp.where(mine, value, jnp.zeros_like(value)), axis)  71.9 us
    reduce_scatter x1, waiting for transfers between devices, per_device(): lax.psum_scatter(exchange_quad, 'col', scatter_dimension=1, tiled=True)  35.3 us
    all_gather x1, waiting for transfers between devices, per_device(): lax.all_gather(exchange_diag.astype(jnp.bfloat16), 'col', axis=1, tiled=T...  26.5 us
    dot_general x4, matrix products, per_device(): lax.dot_general(half_product, aux_block, (((1,), (1,)), ((), ())), prefer...  9.58 us
    dot_general x2, matrix products, per_device(): jnp.dot(fock_part, dens_rows, preferred_element_type=jnp.float32)  4.42 us
    unnamed x10, local copies, waits for them, and re-layouts  3.68 us
  transfers between devices with their start and end apart: 3, of which 3 were waited for; matrix products, arithmetic and copies ran while one was open for 0% of the time, Pallas kernels for 0%

commit v1 on v0

--- a/solution.py
+++ b/solution.py
@@ -1,10 +1,17 @@
+import functools
+
 import jax
 import jax.numpy as jnp
 from jax import lax
+from jax.experimental import pallas as pl
+from jax.experimental.pallas import tpu as pltpu
 from jax.sharding import PartitionSpec as P
 
 TILE = 128
 W = 512
+SUP = W // TILE
+HALF = W // 2
+MESH = pl.DeviceIdType.MESH
 
 
 def from_root(value, axis, root):
@@ -102,12 +109,258 @@
     return (exchange_diag, exchange_density)
 
 
+def mask_tile(tile, flag):
+    return (tile.astype(jnp.float32) * flag.astype(jnp.float32)).astype(jnp.bfloat16)
+
+
+def exchange_kernel(
+    scale, listed, density, three_centre, diag_out, fock_out,
+    raw, block, coef, partial, send_1, recv_1, send_2, recv_2, fock,
+    raw_sem, coef_sem, bc_send, bc_recv, rs1_send, rs1_recv, rs2_send, rs2_recv,
+    ag1_send, ag1_recv, ag2_send, ag2_recv,
+):
+    tile_rows, tile_cols = listed.shape
+    groups = tile_rows // SUP
+    aux_count = three_centre.shape[0]
+    row = lax.axis_index("row")
+    me = lax.axis_index("col")
+    x, y = me % 2, me // 2
+    xn, yn = me + 1 - 2 * x, me + 2 - 4 * y
+    first_tile = row * tile_rows
+    owner = first_tile // tile_cols
+    tile_off = first_tile % tile_cols
+    ox, oy = owner % 2, owner // 2
+    rx, ry = (x + ox) % 2, (y + oy) % 2
+    even = (rx + ry + 1) % 2
+    is_owner = rx + ry == 0
+    hop_to = (xn * even + yn * (1 - even), yn * even + xn * (1 - even))
+    last_of = (rx + 2 * (1 - ry) == 0, ry + 2 * (1 - rx) == 0)
+
+    def remote(src, dst, send_sem, recv_sem, target):
+        return pltpu.make_async_remote_copy(
+            src_ref=src, dst_ref=dst, send_sem=send_sem, recv_sem=recv_sem,
+            device_id=(row, target), device_id_type=MESH,
+        )
+
+    def raw_copy(g):
+        columns = pl.ds(pl.multiple_of((tile_off + g * SUP) * TILE, TILE), W)
+        return pltpu.make_async_copy(
+            density.at[pl.ds(g * W, W), columns], raw.at[g], raw_sem.at[g]
+        )
+
+    def coef_copy(q):
+        return pltpu.make_async_copy(three_centre.at[q], coef.at[q], coef_sem.at[q])
+
+    def piece(g, i):
+        part = block.at[g, pl.ds(i * TILE, TILE)]
+        return remote(part, part, bc_send.at[g, i], bc_recv.at[g, i], hop_to[i // (SUP // 2)])
+
+    @pl.when(is_owner)
+    def _():
+        for g in range(groups):
+            raw_copy(g).start()
+
+    barrier = pltpu.get_barrier_semaphore()
+    for neighbour in (xn, yn):
+        pl.semaphore_signal(barrier, inc=1, device_id=(row, neighbour), device_id_type=MESH)
+    for q in range(aux_count):
+        coef_copy(q).start()
+    pl.semaphore_wait(barrier, 2)
+
+    order = [s + h * (SUP // 2) for s in range(SUP // 2) for h in range(2)]
+
+    @pl.when(is_owner)
+    def _():
+        for g in range(groups):
+            raw_copy(g).wait()
+            for i in order:
+                for j in range(SUP):
+                    rows, cols = pl.ds(i * TILE, TILE), pl.ds(j * TILE, TILE)
+                    flag = listed[g * SUP + i, tile_off + g * SUP + j]
+                    block[g, rows, cols] = mask_tile(raw[g, rows, cols], flag)
+                piece(g, i).start()
+
+    @pl.when(jnp.logical_not(is_owner))
+    def _():
+        for g in range(groups):
+            for i in order:
+                @pl.when(jnp.logical_not(last_of[i // (SUP // 2)]))
+                def _():
+                    piece(g, i).wait_recv()
+                    piece(g, i).start()
+
+    for q in range(aux_count):
+        coef_copy(q).wait()
+
+    near = (xn, yn)
+
+    def stage_1(g, h):
+        return remote(send_1.at[g, h], recv_1.at[g, h], rs1_send.at[g, h], rs1_recv.at[g, h], near[h])
+
+    def stage_2(g, h):
+        return remote(
+            send_2.at[g, h], recv_2.at[g, h], rs2_send.at[g, h], rs2_recv.at[g, h], near[1 - h]
+        )
+
+    def columns_of(dev):
+        return pl.ds(pl.multiple_of(dev * TILE, TILE), TILE)
+
+    def gather_1(g, axis):
+        part = fock.at[pl.ds(g * W, W), columns_of(me)]
+        return remote(part, part, ag1_send.at[g, axis], ag1_recv.at[g, axis], near[axis])
+
+    def gather_2(g, axis):
+        part = fock.at[pl.ds(g * W + axis * HALF, HALF), columns_of(near[1 - axis])]
+        return remote(part, part, ag2_send.at[g, axis], ag2_recv.at[g, axis], near[axis])
+
+    def rows_of(h):
+        return pl.ds(h * HALF, HALF)
+
+    far = me + (xn - me) + (yn - me)
+    for g in range(groups):
+        for h in range(2):
+            @pl.when(last_of[h])
+            def _():
+                for s in range(SUP // 2):
+                    piece(g, s + h * (SUP // 2)).wait_recv()
+        for n, q in enumerate(range(g, aux_count, groups)):
+            half = jnp.dot(coef[q], block[g], preferred_element_type=jnp.float32).astype(jnp.bfloat16)
+            term = lax.dot_general(
+                half, coef[q], (((1,), (1,)), ((), ())), preferred_element_type=jnp.float32
+            )
+            if n == 0:
+                partial[g] = term
+            else:
+                partial[g] += term
+        for h in range(2):
+            send_1[g, h, 0] = partial[g, rows_of(h), columns_of(near[h])].astype(jnp.bfloat16)
+            send_1[g, h, 1] = partial[g, rows_of(h), columns_of(far)].astype(jnp.bfloat16)
+            stage_1(g, h).start()
+    for g in range(groups):
+        for h in range(2):
+            stage_1(g, h).wait_recv()
+            send_2[g, h] = (
+                partial[g, rows_of(h), columns_of(near[1 - h])] + recv_1[g, h, 1].astype(jnp.float32)
+            ).astype(jnp.bfloat16)
+            stage_2(g, h).start()
+    for g in range(groups):
+        for h in range(2):
+            stage_2(g, h).wait_recv()
+            total = (
+                partial[g, rows_of(h), columns_of(me)]
+                + recv_1[g, h, 0].astype(jnp.float32)
+                + recv_2[g, h].astype(jnp.float32)
+            ) * scale
+            rows = pl.ds(g * W + h * HALF, HALF)
+            diag_out[rows] = total
+            fock[rows, columns_of(me)] = total.astype(jnp.bfloat16)
+        for axis in range(2):
+            gather_1(g, axis).start()
+    for g in range(groups):
+        for axis in range(2):
+            gather_1(g, 1 - axis).wait_recv()
+            gather_2(g, axis).start()
+    for g in range(groups):
+        for axis in range(2):
+            gather_2(g, axis).wait_recv()
+    fock_out[...] = fock[...]
+    for g in range(groups):
+        for i in range(SUP):
+            @pl.when(jnp.logical_not(last_of[i // (SUP // 2)]))
+            def _():
+                piece(g, i).wait_send()
+        for h in range(2):
+            stage_1(g, h).wait_send()
+            stage_2(g, h).wait_send()
+            gather_1(g, h).wait_send()
+            gather_2(g, h).wait_send()
+
+
+def apply_kernel(listed, fock, density, result, masked):
+    g, n = pl.program_id(0), pl.program_id(1)
+    tiles = density.shape[1] // TILE
+    for i in range(SUP):
+        for j in range(tiles):
+            rows, cols = slice(i * TILE, (i + 1) * TILE), slice(j * TILE, (j + 1) * TILE)
+            masked[rows, cols] = mask_tile(density[rows, cols], listed[g * SUP + i, n * tiles + j])
+    product = jnp.dot(fock[...], masked[...], preferred_element_type=jnp.float32)
+    result[...] = (product * W ** (-0.5)).astype(jnp.bfloat16)
+
+
+def per_device_whole(density, listed, three_centre):
+    rows, cols = density.shape
+    groups = rows // W
+    aux_count = three_centre.shape[0]
+    aux_group = aux_count * lax.axis_size("col") // groups
+    bf16, dma = jnp.bfloat16, pltpu.SemaphoreType.DMA
+    vmem = pl.BlockSpec(memory_space=pltpu.VMEM)
+    anywhere = pl.BlockSpec(memory_space=pl.ANY)
+    diag, fock = pl.pallas_call(
+        functools.partial(exchange_kernel, aux_group ** (-0.5)),
+        out_shape=(
+            jax.ShapeDtypeStruct((rows, TILE), jnp.float32),
+            jax.ShapeDtypeStruct((rows, W), bf16),
+        ),
+        in_specs=[pl.BlockSpec(memory_space=pltpu.SMEM), anywhere, anywhere],
+        out_specs=(vmem, vmem),
+        scratch_shapes=[
+            pltpu.VMEM((groups, W, W), bf16),
+            pltpu.VMEM((groups, W, W), bf16),
+            pltpu.VMEM((aux_count, W, W), bf16),
+            pltpu.VMEM((groups, W, W), jnp.float32),
+            pltpu.VMEM((groups, 2, 2, HALF, TILE), bf16),
+            pltpu.VMEM((groups, 2, 2, HALF, TILE), bf16),
+            pltpu.VMEM((groups, 2, HALF, TILE), bf16),
+            pltpu.VMEM((groups, 2, HALF, TILE), bf16),
+            pltpu.VMEM((rows, W), bf16),
+            dma((groups,)),
+            dma((aux_count,)),
+            dma((groups, SUP)),
+            dma((groups, SUP)),
+        ]
+        + [dma((groups, 2)) for _ in range(8)],
+        compiler_params=pltpu.CompilerParams(collective_id=0, has_side_effects=True),
+    )(listed, density, three_centre)
+    wide = min(cols, 1024)
+    result = pl.pallas_call(
+        apply_kernel,
+        out_shape=jax.ShapeDtypeStruct((rows, cols), bf16),
+        grid=(groups, cols // wide),
+        in_specs=[
+            pl.BlockSpec(memory_space=pltpu.SMEM),
+            pl.BlockSpec((W, W), lambda g, n: (g, 0)),
+            pl.BlockSpec((W, wide), lambda g, n: (g, n)),
+        ],
+        out_specs=pl.BlockSpec((W, wide), lambda g, n: (g, n)),
+        scratch_shapes=[pltpu.VMEM((W, wide), bf16)],
+    )(listed, fock, density)
+    return diag, result
+
+
+def takes_whole(mesh, density, listed, three_centre):
+    row_count, col_count = mesh.shape["row"], mesh.shape["col"]
+    rows = density.shape[0] // row_count
+    cols = density.shape[1] // col_count
+    aux_count = three_centre.shape[0] // (row_count * col_count)
+    if rows % W or cols % rows or col_count != 4 or col_count * TILE != W:
+        return False
+    return aux_count % (rows // W) == 0
+
+
 def solution(mesh):
     placed = (P("row", "col"), P("row", "col"), P(("row", "col"), None, None))
-    return jax.shard_map(
-        per_device,
-        mesh=mesh,
-        in_specs=placed,
-        out_specs=(P("row", "col"), P("row", "col")),
-        check_vma=False,
-    )
+
+    def mapped(body):
+        return jax.shard_map(
+            body,
+            mesh=mesh,
+            in_specs=placed,
+            out_specs=(P("row", "col"), P("row", "col")),
+            check_vma=False,
+        )
+
+    def run(density, listed, three_centre):
+        whole = takes_whole(mesh, density, listed, three_centre)
+        return mapped(per_device_whole if whole else per_device)(density, listed, three_centre)
+
+    return run

time: 178 us -> 56.1 us (0.32)
  waiting for transfers between devices: 134 us -> 0 us
  Pallas kernels: 0 us -> 54.4 us
  matrix products: 14 us -> 0 us
  between operations: 14 us -> 0.65 us
  other arithmetic: 11.1 us -> 0 us
  local copies, waits for them, and re-layouts: 4.68 us -> 0.8 us
    psum x1 -> x0, waiting for transfers between devices: 71.9 us -> none  [from_root(): return lax.psum(jnp.where(mine, value, jnp.zeros_like(value)), axis)]
    pallas_call x0 -> x2, Pallas kernels: none -> 54.4 us  [the longest x1 47.6 us: per_device_whole(): pl.pallas_call(functools.partial(exchange_kernel, aux_group ** (-0.5)), o...]
    reduce_scatter x1 -> x0, waiting for transfers between devices: 35.3 us -> none  [per_device(): lax.psum_scatter(exchange_quad, 'col', scatter_dimension=1, tiled=True)]
    all_gather x1 -> x0, waiting for transfers between devices: 26.5 us -> none  [per_device(): lax.all_gather(exchange_diag.astype(jnp.bfloat16), 'col', axis=1, tiled=T...]
    dot_general x6 -> x0, matrix products: 14 us -> none  [the longest x4 9.58 us: per_device(): lax.dot_general(half_product, aux_block, (((1,), (1,)), ((), ())), prefer...]
    mul x2 -> x0, other arithmetic: 4.19 us -> none  [the longest x1 3.28 us: per_device(): exchange_quad * aux_group ** (-0.5)]
    unnamed x10 -> x3, local copies, waits for them, and re-layouts: 3.68 us -> 0.8 us
    concatenate x1 -> x0, other arithmetic: 2.6 us -> none  [per_device(): exchange_density = jnp.concatenate(products, axis=0).astype(jnp.bfloat16)]
  transfers between devices with their start and end apart: 3 -> 0, of which waited for: 3 -> 0; matrix products, arithmetic and copies ran while one was open for 0% -> 0% of each run, Pallas kernels for 0% -> 0%
where the time goes in v1:
time: 56.1 us; the launch traced here: 55.9 us
  Pallas kernels  54.4 us (97%)
  local copies, waits for them, and re-layouts  0.8 us (1%)
  between operations  0.65 us (1%)
    pallas_call x1, Pallas kernels, per_device_whole(): pl.pallas_call(functools.partial(exchange_kernel, aux_group ** (-0.5)), o...  47.6 us
    pallas_call x1, Pallas kernels, per_device_whole(): pl.pallas_call(apply_kernel, out_shape=jax.ShapeDtypeStruct((rows, cols),...  6.8 us

profile of v1, /device:TPU:0, one launch (start us, length us, event | category | flops | bytes accessed | tf_op | source)
XLA Modules:
  0.0 55.9 jit_solution(12496343093081905785)
XLA Ops:
  0.6 47.6 %shard_map.50 = (f32[1024,128]{1,0:T(8,128)}, bf16[1024,512]{1,0:T(8,128)(2,1)}) custom-call(s32[8,16]{1,0:T(8,128)} %listed.3, bf16[1024,2048]{1,0:T(8,128)(2,1)} %density.3, bf16[4,512,512]{2,1,0:T(8,128)(2,1)} %three_centre.1), custom_call_target="tpu_custom_call" | custom-call | tf_op jit(solution)/shard_map/pallas_call | solution.py:298
  48.2 0.0 copy-start
  48.3 6.8 %shard_map.51 = bf16[1024,2048]{1,0:T(8,128)(2,1)} custom-call(s32[8,16]{1,0:T(8,128)} %listed.3, bf16[1024,512]{1,0:T(8,128)(2,1)} %get-tuple-element.5.fock, bf16[1024,2048]{1,0:T(8,128)(2,1)} %density.3), custom_call_target="tpu_custom_call" | custom-call | tf_op jit(solution)/shard_map/pallas_call | solution.py:325
  55.1 0.0 copy-done
  55.1 0.8 %copy.6 = f32[1024,128]{1,0:T(8,128)} copy(f32[1024,128]{1,0:T(8,128)S(1)} %copy-done) | data formatting | bytes 1048576
Async XLA Ops:
  48.2 6.8 %copy-start = (f32[1024,128]{1,0:T(8,128)S(1)}, f32[1024,128]{1,0:T(8,128)}, u32[]{:S(2)}) copy-start(f32[1024,128]{1,0:T(8,128)} %get-tuple-element.8) | copy-start | bytes 1572868

commit v2 on v1

--- a/solution.py
+++ b/solution.py
@@ -10,7 +10,9 @@
 TILE = 128
 W = 512
 SUP = W // TILE
-HALF = W // 2
+UNIT = W // 2
+PART = UNIT // 2
+PIECE = TILE // 2
 MESH = pl.DeviceIdType.MESH
 
 
@@ -110,22 +112,25 @@
 
 
 def mask_tile(tile, flag):
-    return (tile.astype(jnp.float32) * flag.astype(jnp.float32)).astype(jnp.bfloat16)
+    return tile * jnp.full(tile.shape, flag.astype(jnp.float32)).astype(jnp.bfloat16)
 
 
 def exchange_kernel(
     scale, listed, density, three_centre, diag_out, fock_out,
-    raw, block, coef, partial, send_1, recv_1, send_2, recv_2, fock,
-    raw_sem, coef_sem, bc_send, bc_recv, rs1_send, rs1_recv, rs2_send, rs2_recv,
-    ag1_send, ag1_recv, ag2_send, ag2_recv,
+    raw, block, coef, half, partial, send_1, recv_1, send_2, recv_2, diag, fock,
+    raw_sem, coef_sem, diag_sem, fock_sem, bc_send, bc_recv, rs1_send, rs1_recv,
+    rs2_send, rs2_recv, ag1_send, ag1_recv, ag2_send, ag2_recv,
 ):
     tile_rows, tile_cols = listed.shape
     groups = tile_rows // SUP
+    units = groups * (W // UNIT)
     aux_count = three_centre.shape[0]
     row = lax.axis_index("row")
     me = lax.axis_index("col")
     x, y = me % 2, me // 2
     xn, yn = me + 1 - 2 * x, me + 2 - 4 * y
+    far = xn + yn - me
+    near = (xn, yn)
     first_tile = row * tile_rows
     owner = first_tile // tile_cols
     tile_off = first_tile % tile_cols
@@ -135,6 +140,10 @@
     is_owner = rx + ry == 0
     hop_to = (xn * even + yn * (1 - even), yn * even + xn * (1 - even))
     last_of = (rx + 2 * (1 - ry) == 0, ry + 2 * (1 - rx) == 0)
+    relays_of = (
+        (rx + ry) * (rx + 1 - ry) > 0,
+        (rx + ry) * (ry + 1 - rx) > 0,
+    )
 
     def remote(src, dst, send_sem, recv_sem, target):
         return pltpu.make_async_remote_copy(
@@ -151,9 +160,11 @@
     def coef_copy(q):
         return pltpu.make_async_copy(three_centre.at[q], coef.at[q], coef_sem.at[q])
 
+    per_path = W // PIECE // 2
+
     def piece(g, i):
-        part = block.at[g, pl.ds(i * TILE, TILE)]
-        return remote(part, part, bc_send.at[g, i], bc_recv.at[g, i], hop_to[i // (SUP // 2)])
+        part = block.at[g, pl.ds(i * PIECE, PIECE)]
+        return remote(part, part, bc_send.at[g, i], bc_recv.at[g, i], hop_to[i // per_path])
 
     @pl.when(is_owner)
     def _():
@@ -161,122 +172,149 @@
             raw_copy(g).start()
 
     barrier = pltpu.get_barrier_semaphore()
-    for neighbour in (xn, yn):
+    for neighbour in near:
         pl.semaphore_signal(barrier, inc=1, device_id=(row, neighbour), device_id_type=MESH)
     for q in range(aux_count):
         coef_copy(q).start()
     pl.semaphore_wait(barrier, 2)
 
-    order = [s + h * (SUP // 2) for s in range(SUP // 2) for h in range(2)]
+    order = [s + h * per_path for s in range(per_path) for h in range(2)]
 
     @pl.when(is_owner)
     def _():
         for g in range(groups):
             raw_copy(g).wait()
             for i in order:
+                rows = pl.ds(i * PIECE, PIECE)
                 for j in range(SUP):
-                    rows, cols = pl.ds(i * TILE, TILE), pl.ds(j * TILE, TILE)
-                    flag = listed[g * SUP + i, tile_off + g * SUP + j]
+                    cols = pl.ds(j * TILE, TILE)
+                    flag = listed[g * SUP + i * PIECE // TILE, tile_off + g * SUP + j]
                     block[g, rows, cols] = mask_tile(raw[g, rows, cols], flag)
                 piece(g, i).start()
 
-    @pl.when(jnp.logical_not(is_owner))
-    def _():
-        for g in range(groups):
-            for i in order:
-                @pl.when(jnp.logical_not(last_of[i // (SUP // 2)]))
-                def _():
-                    piece(g, i).wait_recv()
-                    piece(g, i).start()
-
+    def relay(g, pieces):
+        if g == groups:
+            return
+        for i in pieces:
+            @pl.when(relays_of[i // per_path])
+            def _():
+                piece(g, i).wait_recv()
+                piece(g, i).start()
+
+    def stage_1(u, h):
+        return remote(send_1.at[u, h], recv_1.at[u, h], rs1_send.at[u, h], rs1_recv.at[u, h], near[h])
+
+    def stage_2(u, h):
+        return remote(
+            send_2.at[u, h], recv_2.at[u, h], rs2_send.at[u, h], rs2_recv.at[u, h], near[1 - h]
+        )
+
+    def columns_of(dev):
+        return pl.ds(pl.multiple_of(dev * TILE, TILE), TILE)
+
+    def rows_of(u, h):
+        return pl.ds(u * UNIT + h * PART, PART)
+
+    def gather_1(u, axis):
+        part = fock.at[pl.ds(u * UNIT, UNIT), columns_of(me)]
+        return remote(part, part, ag1_send.at[u, axis], ag1_recv.at[u, axis], near[axis])
+
+    def gather_2(u, axis):
+        part = fock.at[rows_of(u, axis), columns_of(near[1 - axis])]
+        return remote(part, part, ag2_send.at[u, axis], ag2_recv.at[u, axis], near[axis])
+
+    def diag_copy(u):
+        rows = pl.ds(u * UNIT, UNIT)
+        return pltpu.make_async_copy(diag.at[rows], diag_out.at[rows], diag_sem.at[u])
+
+    def fock_copy(u):
+        rows = pl.ds(u * UNIT, UNIT)
+        return pltpu.make_async_copy(fock.at[rows], fock_out.at[rows], fock_sem.at[u])
+
+    relay(0, order)
     for q in range(aux_count):
         coef_copy(q).wait()
-
-    near = (xn, yn)
-
-    def stage_1(g, h):
-        return remote(send_1.at[g, h], recv_1.at[g, h], rs1_send.at[g, h], rs1_recv.at[g, h], near[h])
-
-    def stage_2(g, h):
-        return remote(
-            send_2.at[g, h], recv_2.at[g, h], rs2_send.at[g, h], rs2_recv.at[g, h], near[1 - h]
-        )
-
-    def columns_of(dev):
-        return pl.ds(pl.multiple_of(dev * TILE, TILE), TILE)
-
-    def gather_1(g, axis):
-        part = fock.at[pl.ds(g * W, W), columns_of(me)]
-        return remote(part, part, ag1_send.at[g, axis], ag1_recv.at[g, axis], near[axis])
-
-    def gather_2(g, axis):
-        part = fock.at[pl.ds(g * W + axis * HALF, HALF), columns_of(near[1 - axis])]
-        return remote(part, part, ag2_send.at[g, axis], ag2_recv.at[g, axis], near[axis])
-
-    def rows_of(h):
-        return pl.ds(h * HALF, HALF)
-
-    far = me + (xn - me) + (yn - me)
+    quarter = len(order) // 4
     for g in range(groups):
+        members = list(range(g, aux_count, groups))
+        relay(g + 1, order[:quarter])
         for h in range(2):
             @pl.when(last_of[h])
             def _():
-                for s in range(SUP // 2):
-                    piece(g, s + h * (SUP // 2)).wait_recv()
-        for n, q in enumerate(range(g, aux_count, groups)):
-            half = jnp.dot(coef[q], block[g], preferred_element_type=jnp.float32).astype(jnp.bfloat16)
-            term = lax.dot_general(
-                half, coef[q], (((1,), (1,)), ((), ())), preferred_element_type=jnp.float32
-            )
-            if n == 0:
-                partial[g] = term
-            else:
-                partial[g] += term
-        for h in range(2):
-            send_1[g, h, 0] = partial[g, rows_of(h), columns_of(near[h])].astype(jnp.bfloat16)
-            send_1[g, h, 1] = partial[g, rows_of(h), columns_of(far)].astype(jnp.bfloat16)
-            stage_1(g, h).start()
+                for s in range(per_path):
+                    piece(g, s + h * per_path).wait_recv()
+        for n, q in enumerate(members):
+            half[n] = jnp.dot(coef[q], block[g], preferred_element_type=jnp.float32).astype(jnp.bfloat16)
+            if n < 2:
+                relay(g + 1, order[(n + 1) * quarter : (n + 2) * quarter])
+        for v in range(W // UNIT):
+            u = g * (W // UNIT) + v
+            rows = pl.ds(v * UNIT, UNIT)
+            for n, q in enumerate(members):
+                term = lax.dot_general(
+                    half[n, rows], coef[q], (((1,), (1,)), ((), ())),
+                    preferred_element_type=jnp.float32,
+                )
+                if n == 0:
+                    partial[pl.ds(u * UNIT, UNIT)] = term
+                else:
+                    partial[pl.ds(u * UNIT, UNIT)] += term
+            for h in range(2):
+                send_1[u, h, 0] = partial[rows_of(u, h), columns_of(near[h])].astype(jnp.bfloat16)
+                send_1[u, h, 1] = partial[rows_of(u, h), columns_of(far)].astype(jnp.bfloat16)
+                stage_1(u, h).start()
+        relay(g + 1, order[(min(len(members), 2) + 1) * quarter :])
+
+    for step in range(units + 3):
+        if step < units:
+            u = step
+            for h in range(2):
+                stage_1(u, h).wait_recv()
+                send_2[u, h] = (
+                    partial[rows_of(u, h), columns_of(near[1 - h])]
+                    + recv_1[u, h, 1].astype(jnp.float32)
+                ).astype(jnp.bfloat16)
+                stage_2(u, h).start()
+        if 1 <= step <= units:
+            u = step - 1
+            for h in range(2):
+                stage_2(u, h).wait_recv()
+                total = (
+                    partial[rows_of(u, h), columns_of(me)]
+                    + recv_1[u, h, 0].astype(jnp.float32)
+                    + recv_2[u, h].astype(jnp.float32)
+                ) * scale
+                diag[rows_of(u, h)] = total
+                fock[rows_of(u, h), columns_of(me)] = total.astype(jnp.bfloat16)
+            for axis in range(2):
+                gather_1(u, axis).start()
+            diag_copy(u).start()
+        if 2 <= step <= units + 1:
+            u = step - 2
+            for axis in range(2):
+                gather_1(u, 1 - axis).wait_recv()
+                gather_2(u, axis).start()
+        if 3 <= step:
+            u = step - 3
+            for axis in range(2):
+                gather_2(u, axis).wait_recv()
+            fock_copy(u).start()
     for g in range(groups):
-        for h in range(2):
-            stage_1(g, h).wait_recv()
-            send_2[g, h] = (
-                partial[g, rows_of(h), columns_of(near[1 - h])] + recv_1[g, h, 1].astype(jnp.float32)
-            ).astype(jnp.bfloat16)
-            stage_2(g, h).start()
-    for g in range(groups):
-        for h in range(2):
-            stage_2(g, h).wait_recv()
-            total = (
-                partial[g, rows_of(h), columns_of(me)]
-                + recv_1[g, h, 0].astype(jnp.float32)
-                + recv_2[g, h].astype(jnp.float32)
-            ) * scale
-            rows = pl.ds(g * W + h * HALF, HALF)
-            diag_out[rows] = total
-            fock[rows, columns_of(me)] = total.astype(jnp.bfloat16)
-        for axis in range(2):
-            gather_1(g, axis).start()
-    for g in range(groups):
-        for axis in range(2):
-            gather_1(g, 1 - axis).wait_recv()
-            gather_2(g, axis).start()
-    for g in range(groups):
-        for axis in range(2):
-            gather_2(g, axis).wait_recv()
-    fock_out[...] = fock[...]
-    for g in range(groups):
-        for i in range(SUP):
-            @pl.when(jnp.logical_not(last_of[i // (SUP // 2)]))
+        for i in order:
+            @pl.when(jnp.logical_not(last_of[i // per_path]))
             def _():
                 piece(g, i).wait_send()
+    for u in range(units):
         for h in range(2):
-            stage_1(g, h).wait_send()
-            stage_2(g, h).wait_send()
-            gather_1(g, h).wait_send()
-            gather_2(g, h).wait_send()
-
-
-def apply_kernel(listed, fock, density, result, masked):
+            stage_1(u, h).wait_send()
+            stage_2(u, h).wait_send()
+            gather_1(u, h).wait_send()
+            gather_2(u, h).wait_send()
+        diag_copy(u).wait()
+        fock_copy(u).wait()
+
+
+def apply_kernel(listed, fock, density, diag, result, diag_out, masked):
     g, n = pl.program_id(0), pl.program_id(1)
     tiles = density.shape[1] // TILE
     for i in range(SUP):
@@ -286,14 +324,18 @@
     product = jnp.dot(fock[...], masked[...], preferred_element_type=jnp.float32)
     result[...] = (product * W ** (-0.5)).astype(jnp.bfloat16)
 
+    @pl.when(n == 0)
+    def _():
+        diag_out[...] = diag[...]
+
 
 def per_device_whole(density, listed, three_centre):
     rows, cols = density.shape
     groups = rows // W
+    units = rows // UNIT
     aux_count = three_centre.shape[0]
     aux_group = aux_count * lax.axis_size("col") // groups
     bf16, dma = jnp.bfloat16, pltpu.SemaphoreType.DMA
-    vmem = pl.BlockSpec(memory_space=pltpu.VMEM)
     anywhere = pl.BlockSpec(memory_space=pl.ANY)
     diag, fock = pl.pallas_call(
         functools.partial(exchange_kernel, aux_group ** (-0.5)),
@@ -302,38 +344,49 @@
             jax.ShapeDtypeStruct((rows, W), bf16),
         ),
         in_specs=[pl.BlockSpec(memory_space=pltpu.SMEM), anywhere, anywhere],
-        out_specs=(vmem, vmem),
+        out_specs=(anywhere, anywhere),
         scratch_shapes=[
             pltpu.VMEM((groups, W, W), bf16),
             pltpu.VMEM((groups, W, W), bf16),
             pltpu.VMEM((aux_count, W, W), bf16),
-            pltpu.VMEM((groups, W, W), jnp.float32),
-            pltpu.VMEM((groups, 2, 2, HALF, TILE), bf16),
-            pltpu.VMEM((groups, 2, 2, HALF, TILE), bf16),
-            pltpu.VMEM((groups, 2, HALF, TILE), bf16),
-            pltpu.VMEM((groups, 2, HALF, TILE), bf16),
+            pltpu.VMEM((aux_count // groups, W, W), bf16),
+            pltpu.VMEM((rows, W), jnp.float32),
+            pltpu.VMEM((units, 2, 2, PART, TILE), bf16),
+            pltpu.VMEM((units, 2, 2, PART, TILE), bf16),
+            pltpu.VMEM((units, 2, PART, TILE), bf16),
+            pltpu.VMEM((units, 2, PART, TILE), bf16),
+            pltpu.VMEM((rows, TILE), jnp.float32),
             pltpu.VMEM((rows, W), bf16),
             dma((groups,)),
             dma((aux_count,)),
-            dma((groups, SUP)),
-            dma((groups, SUP)),
+            dma((units,)),
+            dma((units,)),
+            dma((groups, W // PIECE)),
+            dma((groups, W // PIECE)),
         ]
-        + [dma((groups, 2)) for _ in range(8)],
+        + [dma((units, 2)) for _ in range(8)],
         compiler_params=pltpu.CompilerParams(collective_id=0, has_side_effects=True),
     )(listed, density, three_centre)
     wide = min(cols, 1024)
-    result = pl.pallas_call(
+    result, diag = pl.pallas_call(
         apply_kernel,
-        out_shape=jax.ShapeDtypeStruct((rows, cols), bf16),
+        out_shape=(
+            jax.ShapeDtypeStruct((rows, cols), bf16),
+            jax.ShapeDtypeStruct((rows, TILE), jnp.float32),
+        ),
         grid=(groups, cols // wide),
         in_specs=[
             pl.BlockSpec(memory_space=pltpu.SMEM),
             pl.BlockSpec((W, W), lambda g, n: (g, 0)),
             pl.BlockSpec((W, wide), lambda g, n: (g, n)),
+            pl.BlockSpec((W, TILE), lambda g, n: (g, 0)),
         ],
-        out_specs=pl.BlockSpec((W, wide), lambda g, n: (g, n)),
+        out_specs=(
+            pl.BlockSpec((W, wide), lambda g, n: (g, n)),
+            pl.BlockSpec((W, TILE), lambda g, n: (g, 0)),
+        ),
         scratch_shapes=[pltpu.VMEM((W, wide), bf16)],
-    )(listed, fock, density)
+    )(listed, fock, density, diag)
     return diag, result
 
 

time: 56.1 us -> 59.9 us (1.068)
  Pallas kernels: 54.4 us -> 59 us
  local copies, waits for them, and re-layouts: 0.8 us -> 0 us
    pallas_call x1, Pallas kernels: 47.6 us -> 52.1 us  [per_device_whole(): pl.pallas_call(functools.partial(exchange_kernel, aux_group ** (-0.5)), o...]
    unnamed x3 -> x0, local copies, waits for them, and re-layouts: 0.8 us -> none
where the time goes in v2:
time: 59.9 us; the launch traced here: 59.7 us
  Pallas kernels  59 us (98%)
  between operations  0.64 us (1%)
    pallas_call x1, Pallas kernels, per_device_whole(): pl.pallas_call(functools.partial(exchange_kernel, aux_group ** (-0.5)), o...  52.1 us
    pallas_call x1, Pallas kernels, per_device_whole(): pl.pallas_call(apply_kernel, out_shape=(jax.ShapeDtypeStruct((rows, cols)...  6.99 us

profile of v2, /device:TPU:0, one launch (start us, length us, event | category | flops | bytes accessed | tf_op | source)
XLA Modules:
  0.0 59.7 jit_solution(3173906577778952351)
XLA Ops:
  0.6 52.1 %shard_map.50 = (f32[1024,128]{1,0:T(8,128)}, bf16[1024,512]{1,0:T(8,128)(2,1)}) custom-call(s32[8,16]{1,0:T(8,128)} %listed.3, bf16[1024,2048]{1,0:T(8,128)(2,1)} %density.3, bf16[4,512,512]{2,1,0:T(8,128)(2,1)} %three_centre.1), custom_call_target="tpu_custom_call" | custom-call | tf_op jit(solution)/shard_map/pallas_call | solution.py:340
  52.7 7.0 %shard_map.51 = (bf16[1024,2048]{1,0:T(8,128)(2,1)}, f32[1024,128]{1,0:T(8,128)}) custom-call(s32[8,16]{1,0:T(8,128)} %listed.3, bf16[1024,512]{1,0:T(8,128)(2,1)} %get-tuple-element.6.fock, bf16[1024,2048]{1,0:T(8,128)(2,1)} %density.3, f32[1024,128]{1,0:T(8,128)} %get-tuple-element.7.diag), custom_call_target="tpu_custom_call" | custom-call | tf_op jit(solution)/shard_map/pallas_call | solution.py:371

commit v3 on v2

--- a/solution.py
+++ b/solution.py
@@ -12,7 +12,8 @@
 SUP = W // TILE
 UNIT = W // 2
 PART = UNIT // 2
-PIECE = TILE // 2
+PIECE = 32
+BAND = 512
 MESH = pl.DeviceIdType.MESH
 
 
@@ -193,8 +194,6 @@
                 piece(g, i).start()
 
     def relay(g, pieces):
-        if g == groups:
-            return
         for i in pieces:
             @pl.when(relays_of[i // per_path])
             def _():
@@ -231,13 +230,12 @@
         rows = pl.ds(u * UNIT, UNIT)
         return pltpu.make_async_copy(fock.at[rows], fock_out.at[rows], fock_sem.at[u])
 
-    relay(0, order)
+    for g in range(groups):
+        relay(g, order)
     for q in range(aux_count):
         coef_copy(q).wait()
-    quarter = len(order) // 4
     for g in range(groups):
         members = list(range(g, aux_count, groups))
-        relay(g + 1, order[:quarter])
         for h in range(2):
             @pl.when(last_of[h])
             def _():
@@ -245,8 +243,6 @@
                     piece(g, s + h * per_path).wait_recv()
         for n, q in enumerate(members):
             half[n] = jnp.dot(coef[q], block[g], preferred_element_type=jnp.float32).astype(jnp.bfloat16)
-            if n < 2:
-                relay(g + 1, order[(n + 1) * quarter : (n + 2) * quarter])
         for v in range(W // UNIT):
             u = g * (W // UNIT) + v
             rows = pl.ds(v * UNIT, UNIT)
@@ -263,10 +259,9 @@
                 send_1[u, h, 0] = partial[rows_of(u, h), columns_of(near[h])].astype(jnp.bfloat16)
                 send_1[u, h, 1] = partial[rows_of(u, h), columns_of(far)].astype(jnp.bfloat16)
                 stage_1(u, h).start()
-        relay(g + 1, order[(min(len(members), 2) + 1) * quarter :])
-
-    for step in range(units + 3):
-        if step < units:
+
+    for phase, step in [(p, u) for p in range(4) for u in range(units)]:
+        if phase == 0:
             u = step
             for h in range(2):
                 stage_1(u, h).wait_recv()
@@ -275,8 +270,8 @@
                     + recv_1[u, h, 1].astype(jnp.float32)
                 ).astype(jnp.bfloat16)
                 stage_2(u, h).start()
-        if 1 <= step <= units:
-            u = step - 1
+        if phase == 1:
+            u = step
             for h in range(2):
                 stage_2(u, h).wait_recv()
                 total = (
@@ -289,13 +284,13 @@
             for axis in range(2):
                 gather_1(u, axis).start()
             diag_copy(u).start()
-        if 2 <= step <= units + 1:
-            u = step - 2
+        if phase == 2:
+            u = step
             for axis in range(2):
                 gather_1(u, 1 - axis).wait_recv()
                 gather_2(u, axis).start()
-        if 3 <= step:
-            u = step - 3
+        if phase == 3:
+            u = step
             for axis in range(2):
                 gather_2(u, axis).wait_recv()
             fock_copy(u).start()
@@ -314,19 +309,51 @@
         fock_copy(u).wait()
 
 
-def apply_kernel(listed, fock, density, diag, result, diag_out, masked):
-    g, n = pl.program_id(0), pl.program_id(1)
-    tiles = density.shape[1] // TILE
-    for i in range(SUP):
-        for j in range(tiles):
-            rows, cols = slice(i * TILE, (i + 1) * TILE), slice(j * TILE, (j + 1) * TILE)
-            masked[rows, cols] = mask_tile(density[rows, cols], listed[g * SUP + i, n * tiles + j])
-    product = jnp.dot(fock[...], masked[...], preferred_element_type=jnp.float32)
-    result[...] = (product * W ** (-0.5)).astype(jnp.bfloat16)
-
-    @pl.when(n == 0)
-    def _():
-        diag_out[...] = diag[...]
+def apply_kernel(
+    listed, fock_in, density, diag_in, result, diag_out, fock, dens, out, diag,
+    fock_sem, dens_sem, out_sem, diag_sem,
+):
+    rows, cols = density.shape
+    groups = rows // W
+
+    def fock_copy(g):
+        part = pl.ds(g * W, W)
+        return pltpu.make_async_copy(fock_in.at[part], fock.at[part], fock_sem.at[g])
+
+    def dens_copy(t):
+        part = pl.ds(t * TILE, TILE)
+        return pltpu.make_async_copy(density.at[part], dens.at[part], dens_sem.at[t])
+
+    def out_copy(m):
+        part = pl.ds(m * BAND, BAND)
+        return pltpu.make_async_copy(out.at[part], result.at[part], out_sem.at[m])
+
+    for g in range(groups):
+        for t in range(g * SUP, (g + 1) * SUP):
+            dens_copy(t).start()
+        fock_copy(g).start()
+    pltpu.make_async_copy(diag_in, diag, diag_sem.at[0]).start()
+    for g in range(groups):
+        for t in range(g * SUP, (g + 1) * SUP):
+            dens_copy(t).wait()
+            part = pl.ds(t * TILE, TILE)
+            for j in range(cols // TILE):
+                span = pl.ds(j * TILE, TILE)
+                dens[part, span] = mask_tile(dens[part, span], listed[t, j])
+        fock_copy(g).wait()
+        if g == 0:
+            pltpu.make_async_copy(diag_in, diag, diag_sem.at[0]).wait()
+            pltpu.make_async_copy(diag, diag_out, diag_sem.at[1]).start()
+        for m in range(g * W // BAND, (g + 1) * W // BAND):
+            part = pl.ds(m * BAND, BAND)
+            product = jnp.dot(
+                fock[part], dens[pl.ds(g * W, W)], preferred_element_type=jnp.float32
+            )
+            out[part] = (product * W ** (-0.5)).astype(jnp.bfloat16)
+            out_copy(m).start()
+    for m in range(rows // BAND):
+        out_copy(m).wait()
+    pltpu.make_async_copy(diag, diag_out, diag_sem.at[1]).wait()
 
 
 def per_device_whole(density, listed, three_centre):
@@ -367,25 +394,24 @@
         + [dma((units, 2)) for _ in range(8)],
         compiler_params=pltpu.CompilerParams(collective_id=0, has_side_effects=True),
     )(listed, density, three_centre)
-    wide = min(cols, 1024)
     result, diag = pl.pallas_call(
         apply_kernel,
         out_shape=(
             jax.ShapeDtypeStruct((rows, cols), bf16),
             jax.ShapeDtypeStruct((rows, TILE), jnp.float32),
         ),
-        grid=(groups, cols // wide),
-        in_specs=[
-            pl.BlockSpec(memory_space=pltpu.SMEM),
-            pl.BlockSpec((W, W), lambda g, n: (g, 0)),
-            pl.BlockSpec((W, wide), lambda g, n: (g, n)),
-            pl.BlockSpec((W, TILE), lambda g, n: (g, 0)),
+        in_specs=[pl.BlockSpec(memory_space=pltpu.SMEM), anywhere, anywhere, anywhere],
+        out_specs=(anywhere, anywhere),
+        scratch_shapes=[
+            pltpu.VMEM((rows, W), bf16),
+            pltpu.VMEM((rows, cols), bf16),
+            pltpu.VMEM((rows, cols), bf16),
+            pltpu.VMEM((rows, TILE), jnp.float32),
+            dma((groups,)),
+            dma((rows // TILE,)),
+            dma((rows // BAND,)),
+            dma((2,)),
         ],
-        out_specs=(
-            pl.BlockSpec((W, wide), lambda g, n: (g, n)),
-            pl.BlockSpec((W, TILE), lambda g, n: (g, 0)),
-        ),
-        scratch_shapes=[pltpu.VMEM((W, wide), bf16)],
     )(listed, fock, density, diag)
     return diag, result
 

time: 59.9 us -> 51.4 us (0.86)
  Pallas kernels: 59 us -> 50.5 us
    pallas_call x1, Pallas kernels: 52.1 us -> 42.7 us  [per_device_whole(): pl.pallas_call(functools.partial(exchange_kernel, aux_group ** (-0.5)), o...]
    pallas_call x1, Pallas kernels: 6.99 us -> 7.8 us  [per_device_whole(): pl.pallas_call(apply_kernel, out_shape=(jax.ShapeDtypeStruct((rows, cols)...]
where the time goes in v3:
time: 51.4 us; the launch traced here: 51.1 us
  Pallas kernels  50.5 us (98%)
  between operations  0.64 us (1%)
    pallas_call x1, Pallas kernels, per_device_whole(): pl.pallas_call(functools.partial(exchange_kernel, aux_group ** (-0.5)), o...  42.7 us
    pallas_call x1, Pallas kernels, per_device_whole(): pl.pallas_call(apply_kernel, out_shape=(jax.ShapeDtypeStruct((rows, cols)...  7.8 us

profile of v3, /device:TPU:0, one launch (start us, length us, event | category | flops | bytes accessed | tf_op | source)
XLA Modules:
  0.0 51.1 jit_solution(2845896650031724481)
XLA Ops:
  0.6 42.7 %shard_map.50 = (f32[1024,128]{1,0:T(8,128)}, bf16[1024,512]{1,0:T(8,128)(2,1)}) custom-call(s32[8,16]{1,0:T(8,128)} %listed.3, bf16[1024,2048]{1,0:T(8,128)(2,1)} %density.3, bf16[4,512,512]{2,1,0:T(8,128)(2,1)} %three_centre.1), custom_call_target="tpu_custom_call" | custom-call | tf_op jit(solution)/shard_map/pallas_call | solution.py:367
  43.3 7.8 %shard_map.51 = (bf16[1024,2048]{1,0:T(8,128)(2,1)}, f32[1024,128]{1,0:T(8,128)}) custom-call(s32[8,16]{1,0:T(8,128)} %listed.3, bf16[1024,512]{1,0:T(8,128)(2,1)} %get-tuple-element.6.fock_in, bf16[1024,2048]{1,0:T(8,128)(2,1)} %density.3, f32[1024,128]{1,0:T(8,128)} %get-tuple-element.7.diag_in), custom_call_target="tpu_custom_call" | custom-call | tf_op jit(solution)/shard_map/pallas_call | solution.py:397

commit v4 on v3

--- a/solution.py
+++ b/solution.py
@@ -13,7 +13,7 @@
 UNIT = W // 2
 PART = UNIT // 2
 PIECE = 32
-BAND = 512
+BAND = 256
 MESH = pl.DeviceIdType.MESH
 
 
@@ -117,7 +117,8 @@
 
 
 def exchange_kernel(
-    scale, listed, density, three_centre, diag_out, fock_out,
+    scale, listed, density, three_centre, diag_out, fock_out, masked_out,
+    dens, dens_sem, masked_sem,
     raw, block, coef, half, partial, send_1, recv_1, send_2, recv_2, diag, fock,
     raw_sem, coef_sem, diag_sem, fock_sem, bc_send, bc_recv, rs1_send, rs1_recv,
     rs2_send, rs2_recv, ag1_send, ag1_recv, ag2_send, ag2_recv,
@@ -172,11 +173,21 @@
         for g in range(groups):
             raw_copy(g).start()
 
+    def dens_copy(t):
+        part = pl.ds(t * TILE, TILE)
+        return pltpu.make_async_copy(density.at[part], dens.at[part], dens_sem.at[t])
+
+    def masked_copy(t):
+        part = pl.ds(t * TILE, TILE)
+        return pltpu.make_async_copy(dens.at[part], masked_out.at[part], masked_sem.at[t])
+
     barrier = pltpu.get_barrier_semaphore()
     for neighbour in near:
         pl.semaphore_signal(barrier, inc=1, device_id=(row, neighbour), device_id_type=MESH)
     for q in range(aux_count):
         coef_copy(q).start()
+    for t in range(tile_rows):
+        dens_copy(t).start()
     pl.semaphore_wait(barrier, 2)
 
     order = [s + h * per_path for s in range(per_path) for h in range(2)]
@@ -232,6 +243,13 @@
 
     for g in range(groups):
         relay(g, order)
+    for t in range(tile_rows):
+        dens_copy(t).wait()
+        part = pl.ds(t * TILE, TILE)
+        for j in range(tile_cols):
+            span = pl.ds(j * TILE, TILE)
+            dens[part, span] = mask_tile(dens[part, span], listed[t, j])
+        masked_copy(t).start()
     for q in range(aux_count):
         coef_copy(q).wait()
     for g in range(groups):
@@ -307,53 +325,27 @@
             gather_2(u, h).wait_send()
         diag_copy(u).wait()
         fock_copy(u).wait()
-
-
-def apply_kernel(
-    listed, fock_in, density, diag_in, result, diag_out, fock, dens, out, diag,
-    fock_sem, dens_sem, out_sem, diag_sem,
-):
-    rows, cols = density.shape
-    groups = rows // W
-
-    def fock_copy(g):
-        part = pl.ds(g * W, W)
-        return pltpu.make_async_copy(fock_in.at[part], fock.at[part], fock_sem.at[g])
-
-    def dens_copy(t):
-        part = pl.ds(t * TILE, TILE)
-        return pltpu.make_async_copy(density.at[part], dens.at[part], dens_sem.at[t])
+    for t in range(tile_rows):
+        masked_copy(t).wait()
+
+
+def apply_kernel(fock, masked, diag, result, diag_out, out, out_sem, diag_sem):
+    rows = masked.shape[0]
 
     def out_copy(m):
         part = pl.ds(m * BAND, BAND)
         return pltpu.make_async_copy(out.at[part], result.at[part], out_sem.at[m])
 
-    for g in range(groups):
-        for t in range(g * SUP, (g + 1) * SUP):
-            dens_copy(t).start()
-        fock_copy(g).start()
-    pltpu.make_async_copy(diag_in, diag, diag_sem.at[0]).start()
-    for g in range(groups):
-        for t in range(g * SUP, (g + 1) * SUP):
-            dens_copy(t).wait()
-            part = pl.ds(t * TILE, TILE)
-            for j in range(cols // TILE):
-                span = pl.ds(j * TILE, TILE)
-                dens[part, span] = mask_tile(dens[part, span], listed[t, j])
-        fock_copy(g).wait()
-        if g == 0:
-            pltpu.make_async_copy(diag_in, diag, diag_sem.at[0]).wait()
-            pltpu.make_async_copy(diag, diag_out, diag_sem.at[1]).start()
-        for m in range(g * W // BAND, (g + 1) * W // BAND):
-            part = pl.ds(m * BAND, BAND)
-            product = jnp.dot(
-                fock[part], dens[pl.ds(g * W, W)], preferred_element_type=jnp.float32
-            )
-            out[part] = (product * W ** (-0.5)).astype(jnp.bfloat16)
-            out_copy(m).start()
+    pltpu.make_async_copy(diag, diag_out, diag_sem.at[0]).start()
+    for m in range(rows // BAND):
+        part = pl.ds(m * BAND, BAND)
+        support = pl.ds(m * BAND // W * W, W)
+        product = jnp.dot(fock[part], masked[support], preferred_element_type=jnp.float32)
+        out[part] = (product * W ** (-0.5)).astype(jnp.bfloat16)
+        out_copy(m).start()
     for m in range(rows // BAND):
         out_copy(m).wait()
-    pltpu.make_async_copy(diag, diag_out, diag_sem.at[1]).wait()
+    pltpu.make_async_copy(diag, diag_out, diag_sem.at[0]).wait()
 
 
 def per_device_whole(density, listed, three_centre):
@@ -363,16 +355,21 @@
     aux_count = three_centre.shape[0]
     aux_group = aux_count * lax.axis_size("col") // groups
     bf16, dma = jnp.bfloat16, pltpu.SemaphoreType.DMA
+    inside = pl.BlockSpec(memory_space=pltpu.VMEM)
     anywhere = pl.BlockSpec(memory_space=pl.ANY)
-    diag, fock = pl.pallas_call(
+    diag, fock, masked = pl.pallas_call(
         functools.partial(exchange_kernel, aux_group ** (-0.5)),
         out_shape=(
             jax.ShapeDtypeStruct((rows, TILE), jnp.float32),
             jax.ShapeDtypeStruct((rows, W), bf16),
+            jax.ShapeDtypeStruct((rows, cols), bf16),
         ),
         in_specs=[pl.BlockSpec(memory_space=pltpu.SMEM), anywhere, anywhere],
-        out_specs=(anywhere, anywhere),
+        out_specs=(anywhere, anywhere, anywhere),
         scratch_shapes=[
+            pltpu.VMEM((rows, cols), bf16),
+            dma((rows // TILE,)),
+            dma((rows // TILE,)),
             pltpu.VMEM((groups, W, W), bf16),
             pltpu.VMEM((groups, W, W), bf16),
             pltpu.VMEM((aux_count, W, W), bf16),
@@ -392,7 +389,9 @@
             dma((groups, W // PIECE)),
         ]
         + [dma((units, 2)) for _ in range(8)],
-        compiler_params=pltpu.CompilerParams(collective_id=0, has_side_effects=True),
+        compiler_params=pltpu.CompilerParams(
+            collective_id=0, has_side_effects=True, vmem_limit_bytes=24 * 2**20
+        ),
     )(listed, density, three_centre)
     result, diag = pl.pallas_call(
         apply_kernel,
@@ -400,19 +399,15 @@
             jax.ShapeDtypeStruct((rows, cols), bf16),
             jax.ShapeDtypeStruct((rows, TILE), jnp.float32),
         ),
-        in_specs=[pl.BlockSpec(memory_space=pltpu.SMEM), anywhere, anywhere, anywhere],
+        in_specs=[inside, inside, inside],
         out_specs=(anywhere, anywhere),
         scratch_shapes=[
-            pltpu.VMEM((rows, W), bf16),
             pltpu.VMEM((rows, cols), bf16),
-            pltpu.VMEM((rows, cols), bf16),
-            pltpu.VMEM((rows, TILE), jnp.float32),
-            dma((groups,)),
-            dma((rows // TILE,)),
             dma((rows // BAND,)),
-            dma((2,)),
+            dma((1,)),
         ],
-    )(listed, fock, density, diag)
+        compiler_params=pltpu.CompilerParams(vmem_limit_bytes=20 * 2**20),
+    )(fock, masked, diag)
     return diag, result
 
 

time: 51.4 us -> 51.4 us (level)
  local copies, waits for them, and re-layouts: 0 us -> 4.46 us
  Pallas kernels: 50.5 us -> 46.1 us
    unnamed x0 -> x6, local copies, waits for them, and re-layouts: none -> 4.46 us
    pallas_call x1, Pallas kernels: 7.8 us -> 3.37 us  [per_device_whole(): pl.pallas_call(apply_kernel, out_shape=(jax.ShapeDtypeStruct((rows, cols)...]
where the time goes in v4:
time: 51.4 us; the launch traced here: 51.2 us
  Pallas kernels  46.1 us (90%)
  local copies, waits for them, and re-layouts  4.46 us (9%)
  between operations  0.65 us (1%)
    pallas_call x1, Pallas kernels, per_device_whole(): pl.pallas_call(functools.partial(exchange_kernel, aux_group ** (-0.5)), o...  42.8 us
    unnamed x6, local copies, waits for them, and re-layouts  4.46 us
    pallas_call x1, Pallas kernels, per_device_whole(): pl.pallas_call(apply_kernel, out_shape=(jax.ShapeDtypeStruct((rows, cols)...  3.37 us

profile of v4, /device:TPU:0, one launch (start us, length us, event | category | flops | bytes accessed | tf_op | source)
XLA Modules:
  0.0 51.2 jit_solution(3882845991622671806)
XLA Ops:
  0.6 0.0 copy-start
  0.6 2.2 %copy-done = bf16[1024,2048]{1,0:T(8,128)(2,1)S(1)} copy-done((bf16[1024,2048]{1,0:T(8,128)(2,1)S(1)}, bf16[1024,2048]{1,0:T(8,128)(2,1)}, u32[]{:S(2)}) %copy-start) | copy-done | bytes 4194328
  2.8 0.0 copy-start.1
  2.8 1.6 %copy-done.1 = bf16[4,512,512]{2,1,0:T(8,128)(2,1)S(1)} copy-done((bf16[4,512,512]{2,1,0:T(8,128)(2,1)S(1)}, bf16[4,512,512]{2,1,0:T(8,128)(2,1)}, u32[]{:S(2)}) %copy-start.1) | copy-done | bytes 2097176
  4.4 0.0 copy-start.2
  4.4 0.7 %copy-done.2 = s32[8,16]{1,0:T(8,128)S(1)} copy-done((s32[8,16]{1,0:T(8,128)S(1)}, s32[8,16]{1,0:T(8,128)}, u32[]{:S(2)}) %copy-start.2) | copy-done | bytes 536
  5.1 42.8 %shard_map.50 = (f32[1024,128]{1,0:T(8,128)S(1)}, bf16[1024,512]{1,0:T(8,128)(2,1)S(1)}, bf16[1024,2048]{1,0:T(8,128)(2,1)S(1)}) custom-call(s32[8,16]{1,0:T(8,128)S(1)} %copy-done.2, bf16[1024,2048]{1,0:T(8,128)(2,1)S(1)} %copy-done, bf16[4,512,512]{2,1,0:T(8,128)(2,1)S(1)} %copy-done.1), custom_call_target="tpu_custom_call" | custom-call | tf_op jit(solution)/shard_map/pallas_call | solution.py:360
  47.9 3.4 %shard_map.51 = (bf16[1024,2048]{1,0:T(8,128)(2,1)}, f32[1024,128]{1,0:T(8,128)}) custom-call(bf16[1024,512]{1,0:T(8,128)(2,1)S(1)} %get-tuple-element.7.fock, bf16[1024,2048]{1,0:T(8,128)(2,1)S(1)} %get-tuple-element.8.masked, f32[1024,128]{1,0:T(8,128)S(1)} %get-tuple-element.9.diag), custom_call_target="tpu_custom_call" | custom-call | tf_op jit(solution)/shard_map/pallas_call | solution.py:396
Async XLA Ops:
  0.6 2.2 %copy-start = (bf16[1024,2048]{1,0:T(8,128)(2,1)S(1)}, bf16[1024,2048]{1,0:T(8,128)(2,1)}, u32[]{:S(2)}) copy-start(bf16[1024,2048]{1,0:T(8,128)(2,1)} %density.1) | copy-start | bytes 12582916
  2.8 1.6 %copy-start.1 = (bf16[4,512,512]{2,1,0:T(8,128)(2,1)S(1)}, bf16[4,512,512]{2,1,0:T(8,128)(2,1)}, u32[]{:S(2)}) copy-start(bf16[4,512,512]{2,1,0:T(8,128)(2,1)} %three_centre.1) | copy-start | bytes 6291460
  4.4 0.7 %copy-start.2 = (s32[8,16]{1,0:T(8,128)S(1)}, s32[8,16]{1,0:T(8,128)}, u32[]{:S(2)}) copy-start(s32[8,16]{1,0:T(8,128)} %listed.1) | copy-start | bytes 1540
